TPU v7x, 512 devices: a whole 4x4x16 slice. The times are simulated.
512 devices in a mesh: row: 64 (over z, y), col: 8 (over x, core).
Axes of the slice: x: 4, y: 4, z: 16, core: 2. Of those that a mesh axis runs over, the one named last changes fastest.
Arguments:
- amplitudes: bfloat16 [2048, 16384], P('row', 'col'), may hold values from -6 to 6
- integrals: bfloat16 [2048, 16384], P('col', 'row'), may hold values from -0.125 to 0.125
- amp_mask: int32 [64, 128], replicated, may hold values 0 or 1
- int_mask: int32 [64, 128], replicated, may hold values 0 or 1
Outputs:
- scaled_residual: float32 [16384, 16384], P('col', 'row')
- row_norm: float32 [16384], P('col')
Inputs may be any that keep to these rules, and one draw needn't show every extreme that they name: `amp_mask`: an entry of 1 keeps its tile, 0 drops it. `int_mask`: an entry of 1 keeps its tile, 0 drops it.
All inputs are finite; a program needn't handle non-finite values.
Results may differ from a plain program's by a relative error of at most 0.0003.
Values may be sent and summed in bfloat16 or wider, within the bound.
A program may use at most 64 MiB of HBM per device.

v0:
```python
import jax
import jax.numpy as jnp
from jax import lax
from jax.sharding import PartitionSpec as P

OCC = 128
TILE = 128


def contract(left, right):
    return lax.dot_general(
        left, right, (((0,), (0,)), ((), ())), preferred_element_type=jnp.float32
    )


def row_keep(table, start, count, block):
    blocks = table.shape[0]
    owners = (start + jnp.arange(count, dtype=jnp.int32)) // block
    onehot = (owners[:, None] == jnp.arange(blocks, dtype=jnp.int32)[None, :]).astype(jnp.bfloat16)
    picked = jnp.dot(onehot, table.astype(jnp.bfloat16), preferred_element_type=jnp.float32)
    return jnp.repeat(picked, TILE, axis=1).astype(jnp.bfloat16)


def local(amplitudes, integrals, amp_mask, int_mask):
    block, m_dev = amplitudes.shape
    ab_dev = integrals.shape[1]
    row_place = lax.axis_index("row")
    col_place = lax.axis_index("col")
    m_tiles = m_dev // TILE
    n_tiles = ab_dev // TILE
    occ_dev = m_dev // OCC
    amp_keep = lax.dynamic_slice_in_dim(amp_mask, col_place * m_tiles, m_tiles, 1)
    int_keep = lax.dynamic_slice_in_dim(int_mask, row_place * n_tiles, n_tiles, 1)
    own_amp = amplitudes * row_keep(amp_keep, row_place * block, block, block)
    stacked = own_amp[None]
    whole_int = lax.all_gather(integrals, "col", axis=0, tiled=True)
    whole_int = whole_int * row_keep(int_keep, 0, whole_int.shape[0], block)
    total = contract(lax.all_gather(stacked, "row", axis=1, tiled=True)[0], whole_int)
    cube = total.reshape(occ_dev, OCC, ab_dev)
    moved = lax.all_to_all(cube, "col", split_axis=1, concat_axis=0, tiled=True)
    mirror = moved.transpose(1, 0, 2).reshape(m_dev, ab_dev)
    summed = total + mirror
    squares = lax.psum(jnp.sum(summed * summed, axis=1), "row")
    row_norm = jnp.sqrt(squares / (ab_dev * lax.axis_size("row")) + 1e-06)
    return (summed / row_norm[:, None], row_norm)


def solution(mesh):
    return jax.shard_map(
        local,
        mesh=mesh,
        in_specs=(P("row", "col"), P("col", "row"), P(), P()),
        out_specs=(P("col", "row"), P("col")),
        check_vma=False,
    )
```

profile of v0, /device:TPU:2, one launch (start us, length us, event | category | flops | bytes accessed | tf_op | source)
XLA Modules:
  0.0 403.9 jit_solution(1154354201146444259)
XLA Ops:
  7.2 0.0 all-gather.4.cloned.1.call-start
  7.2 0.7 all-gather.4.cloned.1.call-update
  7.9 0.0 all-gather.6.cloned.1.call-start
  8.0 1.0 convolution_convert_fusion.1
  9.0 0.1 copy.9
  9.1 0.1 broadcast_in_dim.6
  9.2 1.6 bitcast_multiply_fusion.2
  10.8 0.0 all-gather.6.cloned.1.call-update
  10.9 1.3 convolution_convert_fusion
  12.1 0.3 copy.10
  12.4 31.8 %all-gather.4.cloned.1.call-done = bf16[2048,256]{1,0:T(8,128)(2,1)} async-done(((bf16[256,256]{1,0:T(8,128)(2,1)}), bf16[2048,256]{1,0:T(8,128)(2,1)}) %all-gather.4.cloned.1.call-update) | async-done | bytes 1048592 | tf_op jit(solution)/shard_map/all_gather | solution.py:36
  44.2 160.9 %all-gather.6.cloned.1.call-done = bf16[2048,2048]{1,0:T(8,128)(2,1)} async-done(((bf16[32,2048]{1,0:T(8,128)(2,1)}), bf16[2048,2048]{1,0:T(8,128)(2,1)}) %all-gather.6.cloned.1.call-update) | async-done | bytes 8388624 | tf_op jit(solution)/shard_map/all_gather | solution.py:38
  205.1 5.8 %broadcast_in_dim.16 = bf16[2048,2,128]{2,1,0:T(2,128)(2,1)S(1)} broadcast(bf16[2048,2]{1,0:T(8,128)(2,1)S(1)} %copy.10), dimensions={0,1} | broadcast | bytes 1056768 | tf_op jit(solution)/shard_map/broadcast_in_dim | solution.py:21
  210.9 6.1 %fusion = f32[2048,256]{1,0:T(8,128)S(1)} fusion(bf16[2048,2048]{1,0:T(8,128)(2,1)} %all-gather.6.cloned.1.call-done, bf16[2048,256]{1,0:T(8,128)(2,1)} %all-gather.4.cloned.1.call-done, bf16[256,8,2,128]{3,2,1,0:T(2,128)(2,1)S(1)} %bitcast.24), kind=kOutput, calls=%fused_computation.5 | convolution fusion | flops 2148007936 | bytes 12582912 | tf_op jit(solution)/shard_map/dot_general | solution.py:11
  217.0 1.2 copy.11
  218.3 30.6 %all_to_all.18 = f32[16,128,256]{2,0,1:T(8,128)S(1)} all-to-all(f32[16,128,256]{2,0,1:T(8,128)S(1)} %copy.11), channel_id=1, replica_groups=mesh['row'=64,'col'=8] {'col'}, dimensions={1} | all-to-all | bytes 4194304 | tf_op jit(solution)/shard_map/all_to_all | solution.py:40
  248.8 0.2 copy.12
  249.0 0.0 copy-start
  249.0 1.3 copy-done
  250.4 0.4 multiply_reduce_fusion
  250.8 142.9 %psum.7 = f32[2048]{0:T(1024)S(1)} all-reduce(f32[2048]{0:T(1024)S(1)} %multiply_reduce_fusion), channel_id=1, replica_groups=mesh['row'=64,'col'=8] {'row'}, use_global_device_ids=true, to_apply=%region_1.2 | all-reduce | flops 2048 | bytes 16384 | tf_op jit(solution)/shard_map/psum | solution.py:43
  393.8 0.0 copy-start.1
  393.8 3.3 broadcast_divide_fusion
  397.0 0.0 copy-done.1
  (3 shorter events, 0.0 us)
Async XLA Ops:
  7.2 37.0 %all-gather.4.cloned.1.call-start = ((), (), s32[]{:S(2)}) async-start(), calls=%async_computation.1 | async-start | bytes 1179648 | tf_op jit(solution)/shard_map/all_gather | solution.py:36
  7.9 197.2 %all-gather.6.cloned.1.call-start = ((), (), s32[]{:S(2)}) async-start(), calls=%async_computation.2 | async-start | bytes 8519680 | tf_op jit(solution)/shard_map/all_gather | solution.py:38
  249.0 1.3 copy-start
  393.8 3.3 copy-start.1
Sparse Core Ops, SparseCore 0:
  10.1 34.0 all-gather.3
  47.7 157.3 all-gather.5
where the time goes:
time: 404 us
  waiting for transfers between devices  193 us (48%)
  blocking collectives  174 us (43%)
  between operations  14.1 us (3%)
  local copies, waits for them, and re-layouts  9.05 us (2%)
  matrix products  8.42 us (2%)
  other arithmetic  5.29 us (1%)
    all_gather x1, waiting for transfers between devices, local(): lax.all_gather(stacked, 'row', axis=1, tiled=True)[0]  161 us
    psum x1, blocking collectives, local(): squares = lax.psum(jnp.sum(summed * summed, axis=1), 'row')  143 us
    all_gather x1, waiting for transfers between devices, local(): whole_int = lax.all_gather(integrals, 'col', axis=0, tiled=True)  31.8 us
    all_to_all x1, blocking collectives, local(): moved = lax.all_to_all(cube, 'col', split_axis=1, concat_axis=0, tiled=True)  30.6 us
  transfers between devices with their start and end apart: 2, of which 2 were waited for; matrix products, arithmetic and copies ran while one was open for 1% of the time, Pallas kernels for 0%

commit v1 on v0

--- a/solution.py
+++ b/solution.py
@@ -40,7 +40,9 @@
     moved = lax.all_to_all(cube, "col", split_axis=1, concat_axis=0, tiled=True)
     mirror = moved.transpose(1, 0, 2).reshape(m_dev, ab_dev)
     summed = total + mirror
-    squares = lax.psum(jnp.sum(summed * summed, axis=1), "row")
+    block_2 = jnp.sum(summed * summed, axis=1)
+    parts = lax.all_gather(block_2, "row", axis=0, tiled=False)
+    squares = parts.sum(axis=0)
     row_norm = jnp.sqrt(squares / (ab_dev * lax.axis_size("row")) + 1e-06)
     return (summed / row_norm[:, None], row_norm)
 

time: 404 us -> 360 us (0.89)
  blocking collectives: 174 us -> 130 us
    psum x1 -> x0, blocking collectives: 143 us -> none  [local(): squares = lax.psum(jnp.sum(summed * summed, axis=1), 'row')]
    all_gather x0 -> x1, blocking collectives: none -> 99.2 us  [local(): parts = lax.all_gather(block_2, 'row', axis=0, tiled=False)]
where the time goes in v1:
time: 360 us
  waiting for transfers between devices  193 us (54%)
  blocking collectives  130 us (36%)
  between operations  14.1 us (4%)
  local copies, waits for them, and re-layouts  8.72 us (2%)
  matrix products  8.42 us (2%)
  other arithmetic  5.33 us (1%)
    all_gather x1, waiting for transfers between devices, local(): lax.all_gather(stacked, 'row', axis=1, tiled=True)[0]  161 us
    all_gather x1, blocking collectives, local(): parts = lax.all_gather(block_2, 'row', axis=0, tiled=False)  99.2 us
    all_gather x1, waiting for transfers between devices, local(): whole_int = lax.all_gather(integrals, 'col', axis=0, tiled=True)  31.8 us
    all_to_all x1, blocking collectives, local(): moved = lax.all_to_all(cube, 'col', split_axis=1, concat_axis=0, tiled=True)  30.6 us
  transfers between devices with their start and end apart: 2, of which 2 were waited for; matrix products, arithmetic and copies ran while one was open for 1% of the time, Pallas kernels for 0%

profile of v1, /device:TPU:2, one launch (start us, length us, event | category | flops | bytes accessed | tf_op | source)
XLA Modules:
  0.0 359.8 jit_solution(13606656119344552991)
XLA Ops:
  7.2 0.0 all-gather.5.cloned.1.call-start
  7.2 0.7 all-gather.5.cloned.1.call-update
  7.9 0.0 all-gather.7.cloned.1.call-start
  8.0 1.0 convolution_convert_fusion.1
  9.0 0.1 copy.13
  9.1 0.1 broadcast_in_dim.6
  9.2 1.6 bitcast_multiply_fusion.2
  10.8 0.0 all-gather.7.cloned.1.call-update
  10.9 1.3 convolution_convert_fusion
  12.1 0.3 copy.14
  12.4 31.8 %all-gather.5.cloned.1.call-done = bf16[2048,256]{1,0:T(8,128)(2,1)} async-done(((bf16[256,256]{1,0:T(8,128)(2,1)}), bf16[2048,256]{1,0:T(8,128)(2,1)}) %all-gather.5.cloned.1.call-update) | async-done | bytes 1048592 | tf_op jit(solution)/shard_map/all_gather | solution.py:36
  44.2 160.9 %all-gather.7.cloned.1.call-done = bf16[2048,2048]{1,0:T(8,128)(2,1)} async-done(((bf16[32,2048]{1,0:T(8,128)(2,1)}), bf16[2048,2048]{1,0:T(8,128)(2,1)}) %all-gather.7.cloned.1.call-update) | async-done | bytes 8388624 | tf_op jit(solution)/shard_map/all_gather | solution.py:38
  205.1 5.8 %broadcast_in_dim.16 = bf16[2048,2,128]{2,1,0:T(2,128)(2,1)S(1)} broadcast(bf16[2048,2]{1,0:T(8,128)(2,1)S(1)} %copy.14), dimensions={0,1} | broadcast | bytes 1056768 | tf_op jit(solution)/shard_map/broadcast_in_dim | solution.py:21
  210.9 6.1 %fusion = f32[2048,256]{1,0:T(8,128)S(1)} fusion(bf16[2048,2048]{1,0:T(8,128)(2,1)} %all-gather.7.cloned.1.call-done, bf16[2048,256]{1,0:T(8,128)(2,1)} %all-gather.5.cloned.1.call-done, bf16[256,8,2,128]{3,2,1,0:T(2,128)(2,1)S(1)} %bitcast.24), kind=kOutput, calls=%fused_computation.5 | convolution fusion | flops 2148007936 | bytes 12582912 | tf_op jit(solution)/shard_map/dot_general | solution.py:11
  217.0 1.2 copy.15
  218.3 30.6 %all_to_all.18 = f32[16,128,256]{2,0,1:T(8,128)S(1)} all-to-all(f32[16,128,256]{2,0,1:T(8,128)S(1)} %copy.15), channel_id=1, replica_groups=mesh['row'=64,'col'=8] {'col'}, dimensions={1} | all-to-all | bytes 4194304 | tf_op jit(solution)/shard_map/all_to_all | solution.py:40
  248.8 0.2 copy.16
  249.0 0.0 copy-start
  249.0 0.4 multiply_reduce_fusion
  249.5 0.9 copy-done
  250.4 99.2 %all-gather.1 = f32[131072]{0:T(1024)S(1)} all-gather(f32[2048]{0:T(1024)S(1)} %multiply_reduce_fusion), channel_id=3, replica_groups=mesh['row'=64,'col'=8] {'row'}, dimensions={0}, use_global_device_ids=true | all-gather | bytes 532480 | tf_op jit(solution)/shard_map/all_gather | solution.py:44
  349.5 0.1 reshape.54
  349.7 0.0 copy-start.1
  349.7 3.3 broadcast_divide_fusion
  353.0 0.0 copy-done.1
  (4 shorter events, 0.1 us)
Async XLA Ops:
  7.2 37.0 %all-gather.5.cloned.1.call-start = ((), (), s32[]{:S(2)}) async-start(), calls=%async_computation.1 | async-start | bytes 1179648 | tf_op jit(solution)/shard_map/all_gather | solution.py:36
  7.9 197.2 %all-gather.7.cloned.1.call-start = ((), (), s32[]{:S(2)}) async-start(), calls=%async_computation.2 | async-start | bytes 8519680 | tf_op jit(solution)/shard_map/all_gather | solution.py:38
  249.0 1.3 copy-start
  349.7 3.3 copy-start.1
Sparse Core Ops, SparseCore 0:
  10.1 34.0 all-gather.4
  47.7 157.3 all-gather.6
